TPU v7x, 128 devices: a whole 4x4x4 slice. The times are simulated.
128 devices in a mesh: ent: 32 (over x_hi, z, y), sec: 4 (over x_lo, core).
Axes of the slice: x: 4 (x_hi: 2, x_lo: 2; x = x_hi * 2 + x_lo), y: 4, z: 4, core: 2. Of those that a mesh axis runs over, the one named last changes fastest.
Arguments:
- features: bfloat16 [4096, 256], P('ent'), may hold values from -6 to 6
- theta: bfloat16 [256, 256], replicated, may hold values from -3 to 3
- section_weight: float32 [65536], P(('ent', 'sec')), may hold values from 0.5 to 2
- pair_rows: int32 [128, 32, 512], P(('ent', 'sec')), may hold values from 0 to 511
- pair_cols: int32 [128, 32, 512], P(('ent', 'sec')), may hold values from 0 to 127
- pair_counts: int32 [128, 32], P(('ent', 'sec')), may hold values from 0 to 512, as said below
- cotangent: bfloat16 [4096, 256], P('ent'), may hold values from -24 to 24
Outputs:
- activated: bfloat16 [4096, 256], P('ent')
- grad_features: bfloat16 [4096, 256], P('ent')
- grad_theta: float32 [256, 256], replicated
- grad_weight: float32 [65536], P(('ent', 'sec'))
Inputs may be any that keep to these rules, and one draw needn't show every extreme that they name: Only the first pair_counts[k, j] slots of shard k and block j are used; some shard uses all 512 slots of some block.
All inputs are finite; a program needn't handle non-finite values.
Results may differ from a plain program's by a relative error of at most 0.0059.
Values may be sent and summed in bfloat16 or wider, within the bound.
A program may use at most 64 MiB of HBM per device.

v0:
```python
import jax
import jax.numpy as jnp
from jax import lax
from jax.sharding import PartitionSpec as P


def hot_table(indices, live_slots, offset, table_width):
    hits = (indices - offset)[:, None] == jnp.arange(table_width, dtype=jnp.int32)[None, :]
    return (hits & live_slots[:, None]).astype(jnp.bfloat16)


def body(features, theta, section_weight, pair_rows, pair_cols, pair_counts, cotangent):
    ent_dev = features.shape[0]
    feature_width = features.shape[1]
    sec_dev = section_weight.shape[0]
    blocks_count = pair_rows.shape[1]
    slot_count = pair_rows.shape[2]
    own_block = lax.axis_index("ent")
    row_lists = pair_rows[0]
    col_lists = pair_cols[0]
    usable = jnp.arange(slot_count, dtype=jnp.int32)[None, :] < pair_counts[0][:, None]
    usable_float = usable.astype(jnp.float32)
    entity_index = jnp.arange(blocks_count, dtype=jnp.int32)[:, None] * ent_dev + col_lists
    local_degree = jax.ops.segment_sum(
        usable_float.reshape(-1), entity_index.reshape(-1), num_segments=blocks_count * ent_dev
    )
    entity_degree = lax.psum(local_degree, ("ent", "sec"))
    own_degree = lax.dynamic_slice_in_dim(entity_degree, own_block * ent_dev, ent_dev)
    entity_scale = lax.rsqrt(1.0 + own_degree)[:, None]
    sec_count = jax.ops.segment_sum(
        usable_float.reshape(-1), row_lists.reshape(-1), num_segments=sec_dev
    )
    section_scale = (section_weight / (1.0 + sec_count))[:, None]

    def entity_fold(running, incoming, start_row):
        row_count = incoming.shape[0]
        span_width = min(row_count, ent_dev)
        block_span = max(row_count // ent_dev, 1)
        offset = start_row

        def add_block(turn_index, accum):
            row_slots = lax.dynamic_index_in_dim(row_lists, turn_index, 0, keepdims=False)
            col_slots = lax.dynamic_index_in_dim(col_lists, turn_index, 0, keepdims=False)
            live_slots = lax.dynamic_index_in_dim(usable, turn_index, 0, keepdims=False)
            values = lax.dynamic_slice_in_dim(incoming, turn_index * span_width, span_width, 0)
            col_hot = hot_table(col_slots, live_slots, offset, span_width)
            row_hot = hot_table(row_slots, live_slots, 0, sec_dev)
            picked = jnp.dot(col_hot, values, preferred_element_type=jnp.float32).astype(
                jnp.bfloat16
            )
            return accum + jnp.einsum(
                "ps,pf->sf", row_hot, picked, preferred_element_type=jnp.float32
            )

        return lax.fori_loop(0, block_span, add_block, running)

    def entity_terms(messages, start_row):
        span_width = min(lax.axis_size("ent") * ent_dev, ent_dev)
        block_span = max(lax.axis_size("ent") * ent_dev // ent_dev, 1)
        offset = start_row

        def block_term(turn_index):
            row_slots = lax.dynamic_index_in_dim(row_lists, turn_index, 0, keepdims=False)
            col_slots = lax.dynamic_index_in_dim(col_lists, turn_index, 0, keepdims=False)
            live_slots = lax.dynamic_index_in_dim(usable, turn_index, 0, keepdims=False)
            row_hot = hot_table(row_slots, live_slots, 0, sec_dev)
            col_hot = hot_table(col_slots, live_slots, offset, span_width)
            picked = jnp.dot(row_hot, messages, preferred_element_type=jnp.float32).astype(
                jnp.bfloat16
            )
            return jnp.einsum("pw,pf->wf", col_hot, picked, preferred_element_type=jnp.float32)

        pieces = lax.map(block_term, jnp.arange(block_span, dtype=jnp.int32))
        return pieces.reshape(block_span * span_width, feature_width)

    def collect(messages):
        partial_sum = lax.psum_scatter(
            entity_terms(messages, jnp.int32(0)), "ent", scatter_dimension=0, tiled=True
        )
        return lax.psum(partial_sum, "sec")

    zero_sections = jnp.zeros((sec_dev, feature_width), jnp.float32)
    projected = jnp.dot(features, theta, preferred_element_type=jnp.float32)
    scaled = (entity_scale * projected).astype(jnp.bfloat16)
    gathered = entity_fold(
        zero_sections, lax.all_gather(scaled, "ent", axis=0, tiled=True), jnp.int32(0)
    )
    messages = (section_scale * gathered).astype(jnp.bfloat16)
    collected = collect(messages)
    preact = entity_scale * collected
    activated = jax.nn.silu(preact).astype(jnp.bfloat16)
    sigmoid_pre = jax.nn.sigmoid(preact)
    grad_pre = cotangent.astype(jnp.float32) * sigmoid_pre * (1.0 + preact * (1.0 - sigmoid_pre))
    back_scaled = (entity_scale * grad_pre).astype(jnp.bfloat16)
    back_gathered = entity_fold(
        zero_sections, lax.all_gather(back_scaled, "ent", axis=0, tiled=True), jnp.int32(0)
    )
    grad_weight = jnp.sum(gathered * back_gathered, axis=1) / (1.0 + sec_count)
    back_messages = (section_scale * back_gathered).astype(jnp.bfloat16)
    back_collected = collect(back_messages)
    grad_proj = (entity_scale * back_collected).astype(jnp.bfloat16)
    grad_features = lax.dot_general(
        grad_proj, theta, (((1,), (1,)), ((), ())), preferred_element_type=jnp.float32
    ).astype(jnp.bfloat16)
    local_theta = lax.dot_general(
        features, grad_proj, (((0,), (0,)), ((), ())), preferred_element_type=jnp.float32
    )
    grad_theta = lax.psum(local_theta, "ent")
    return (activated, grad_features, grad_theta, grad_weight)


def solution(mesh):
    placed = (
        P("ent", None),
        P(),
        P(("ent", "sec")),
        P(("ent", "sec"), None, None),
        P(("ent", "sec"), None, None),
        P(("ent", "sec"), None),
        P("ent", None),
    )
    return jax.shard_map(
        body,
        mesh=mesh,
        in_specs=placed,
        out_specs=(P("ent", None), P("ent", None), P(), P(("ent", "sec"))),
        check_vma=False,
    )
```

profile of v0, /device:TPU:0, one launch (start us, length us, event | category | flops | bytes accessed | tf_op | source)
XLA Modules:
  0.0 1644.0 jit_solution(5554662827985014451)
XLA Ops:
  9.2 113.5 %scatter_custom_fusion = f32[4096]{0:T(1024)S(1)} fusion(s32[16384]{0:T(1024)S(1)} %bitcast.81, f32[16384]{0:T(1024)S(1)} %bitcast.82, f32[]{:T(128)} %constant.131.clone.1), kind=kCustom, calls=%fused_computation.76 | custom fusion | flops 16384 | bytes 16388 | tf_op jit(solution)/shard_map/scatter-add | solution.py:24
  122.6 68.3 %psum.28 = f32[4096]{0:T(1024)S(1)} all-reduce(f32[4096]{0:T(1024)S(1)} %scatter_custom_fusion), channel_id=1, replica_groups=mesh['ent'=32,'sec'=4] {'ent','sec'}, use_global_device_ids=true, to_apply=%region_1.0 | all-reduce | flops 4096 | bytes 32768 | tf_op jit(solution)/shard_map/psum | solution.py:27
  193.5 113.4 %scatter_custom_fusion.1 = f32[512]{0:T(512)S(1)} fusion(s32[16384]{0:T(1024)S(1)} %bitcast.84, f32[16384]{0:T(1024)S(1)} %bitcast.83, f32[]{:T(128)} %constant.137.clone.1), kind=kCustom, calls=%fused_computation.78 | custom fusion | flops 16384 | bytes 2052 | tf_op jit(solution)/shard_map/scatter-add | solution.py:30
  307.7 79.9 %while.50 = (s32[]{:T(128)}, f32[512,256]{1,0:T(8,128)S(1)}, s32[32,512]{1,0:T(8,128)}, pred[32,512]{1,0:T(8,128)(4,1)S(1)}, s32[32,512]{1,0:T(8,128)}, /*index=...) while((s32[]{:T(128)}, f32[512,256]{1,0:T(8,128)S(1)}, ...), condition=%wide.region_4.5_spmd.clone, body=%wide.region_3.4_spmd.clone.sunk | while | flops 168820736 | bytes 1128617 | solution.py:55
  313.4 1.7 convolution_add_fusion.4
  315.9 1.7 convolution_add_fusion.4
  330.9 1.7 convolution_add_fusion.4
  333.4 1.7 convolution_add_fusion.4
  348.4 1.7 convolution_add_fusion.4
  350.9 1.7 convolution_add_fusion.4
  365.9 1.7 convolution_add_fusion.4
  368.4 1.7 convolution_add_fusion.4
  383.4 1.7 convolution_add_fusion.4
  385.9 1.7 convolution_add_fusion.4
  387.7 2.4 broadcast.21.clone
  390.2 144.5 %while.48 = (s32[]{:T(128)}, f32[32,128,256]{2,1,0:T(8,128)}, s32[32]{0:T(128)S(1)}, s32[32,512]{1,0:T(8,128)}, pred[32,512]{1,0:T(8,128)(4,1)S(1)}, /*index=5*/...) while((s32[]{:T(128)}, f32[32,128,256]{2,1,0:T(8,128)}, ...), condition=%wide.region_6.7_spmd, body=%wide.region_5.6_spmd.sunk | while | flops 168558592 | bytes 408219 | solution.py:73
  534.8 188.6 %reduce-scatter.3.cloned.1.call-done = f32[128,256]{1,0:T(8,128)} async-done(((f32[4096,256]{1,0:T(8,128)}), f32[128,256]{1,0:T(8,128)}) %reduce-scatter.3.cloned.1.call-update) | async-done | bytes 131088 | tf_op jit(solution)/shard_map/reduce_scatter | solution.py:77
  723.4 32.8 %all-reduce.4.cloned.1.call-done = f32[128,256]{1,0:T(8,128)} async-done(((f32[128,256]{1,0:T(8,128)}), f32[128,256]{1,0:T(8,128)}) %all-reduce.4.cloned.1.call-update) | async-done | bytes 131088 | tf_op jit(solution)/shard_map/psum | solution.py:80
  756.2 1.7 multiply_convert_fusion.3
  758.0 73.9 %all-gather.5.cloned.1.call-done = bf16[4096,256]{1,0:T(8,128)(2,1)} async-done(((bf16[128,256]{1,0:T(8,128)(2,1)}), bf16[4096,256]{1,0:T(8,128)(2,1)}) %all-gather.5.cloned.1.call-update) | async-done | bytes 2097168 | tf_op jit(solution)/shard_map/all_gather | solution.py:96
  831.9 79.9 %while.51 = (s32[]{:T(128)}, f32[512,256]{1,0:T(8,128)S(1)}, s32[32,512]{1,0:T(8,128)}, pred[32,512]{1,0:T(8,128)(4,1)S(1)}, s32[32,512]{1,0:T(8,128)}, /*index=...) while((s32[]{:T(128)}, f32[512,256]{1,0:T(8,128)S(1)}, ...), condition=%wide.region_10.11_spmd.clone, body=%wide.region_9.10_spmd.clone.sunk | while | flops 168820736 | bytes 1128617 | solution.py:55
  832.6 1.7 convolution_add_fusion.5
  842.6 1.7 convolution_add_fusion.5
  845.1 1.7 convolution_add_fusion.5
  912.0 2.4 broadcast.21
  914.4 144.5 %while.49 = (s32[]{:T(128)}, f32[32,128,256]{2,1,0:T(8,128)}, s32[32]{0:T(128)S(1)}, s32[32,512]{1,0:T(8,128)}, pred[32,512]{1,0:T(8,128)(4,1)S(1)}, /*index=5*/...) while((s32[]{:T(128)}, f32[32,128,256]{2,1,0:T(8,128)}, ...), condition=%wide.region_12.13_spmd, body=%wide.region_11.12_spmd.sunk | while | flops 168558592 | bytes 408219 | solution.py:73
  1059.0 190.6 %reduce-scatter.5.cloned.1.call-done = f32[128,256]{1,0:T(8,128)} async-done(((f32[4096,256]{1,0:T(8,128)}), f32[128,256]{1,0:T(8,128)}) %reduce-scatter.5.cloned.1.call-update) | async-done | bytes 131088 | tf_op jit(solution)/shard_map/reduce_scatter | solution.py:77
  1249.7 32.8 %all-reduce.6.cloned.1.call-done = f32[128,256]{1,0:T(8,128)} async-done(((f32[128,256]{1,0:T(8,128)}), f32[128,256]{1,0:T(8,128)}) %all-reduce.6.cloned.1.call-update) | async-done | bytes 131088 | tf_op jit(solution)/shard_map/psum | solution.py:80
  1282.5 1.9 convolution_bitcast_fusion
  1285.0 1.7 convolution_convert_fusion.4
  1286.8 348.6 %all-reduce.8.cloned.1.call-done = f32[256,256]{0,1:T(8,128)} async-done(((f32[256,256]{0,1:T(8,128)}), f32[256,256]{0,1:T(8,128)}) %all-reduce.8.cloned.1.call-update) | async-done | bytes 262160 | tf_op jit(solution)/shard_map/psum | solution.py:108
  1635.4 1.8 copy.11
  (474 shorter events, 307.0 us)
Async XLA Ops:
  7.2 183.8 %copy-start = (bf16[256,256]{1,0:T(8,128)(2,1)S(1)}, bf16[256,256]{1,0:T(8,128)(2,1)}, u32[]{:S(2)}) copy-start(bf16[256,256]{1,0:T(8,128)(2,1)} %param.16) | copy-start | bytes 393220
  7.2 300.5 %all-gather.3.cloned.1.call-start = ((), (), s32[]{:S(2)}) async-start(), calls=%async_computation.2 | async-start | bytes 2162688 | tf_op jit(solution)/shard_map/all_gather | solution.py:86
  192.6 530.7 %reduce-scatter.3.cloned.1.call-start = ((), (), s32[]{:S(2)}) async-start(), calls=%async_computation.3 | async-start | bytes 4325376 | tf_op jit(solution)/shard_map/reduce_scatter | solution.py:77
  390.1 366.0 %copy-start.2 = (bf16[128,256]{1,0:T(8,128)(2,1)S(1)}, bf16[128,256]{1,0:T(8,128)(2,1)}, u32[]{:S(2)}) copy-start(bf16[128,256]{1,0:T(8,128)(2,1)} %param.21) | copy-start | bytes 196612
  534.7 221.5 %all-reduce.4.cloned.1.call-start = ((), (), s32[]{:S(2)}) async-start(), calls=%async_computation.4 | async-start | bytes 262144 | tf_op jit(solution)/shard_map/psum | solution.py:80
  723.4 108.5 %all-gather.5.cloned.1.call-start = ((), (), s32[]{:S(2)}) async-start(), calls=%async_computation.5 | async-start | bytes 2162688 | tf_op jit(solution)/shard_map/all_gather | solution.py:96
  757.9 491.7 %reduce-scatter.5.cloned.1.call-start = ((), (), s32[]{:S(2)}) async-start(), calls=%async_computation.6 | async-start | bytes 4325376 | tf_op jit(solution)/shard_map/reduce_scatter | solution.py:77
  914.4 368.1 %copy-start.1 = (bf16[128,256]{1,0:T(8,128)(2,1)S(1)}, bf16[128,256]{1,0:T(8,128)(2,1)}, u32[]{:S(2)}) copy-start(bf16[128,256]{1,0:T(8,128)(2,1)} %param.15) | copy-start | bytes 196612
  1059.0 223.6 %all-reduce.6.cloned.1.call-start = ((), (), s32[]{:S(2)}) async-start(), calls=%async_computation.7 | async-start | bytes 262144 | tf_op jit(solution)/shard_map/psum | solution.py:80
  1249.7 385.8 %all-reduce.8.cloned.1.call-start = ((), (), s32[]{:S(2)}) async-start(), calls=%async_computation.8 | async-start | bytes 524288 | tf_op jit(solution)/shard_map/psum | solution.py:108
Sparse Core Ops, SparseCore 0:
  192.7 66.8 all-gather.2
  534.8 188.4 reduce-scatter.2
  725.8 30.3 all-reduce.3
  760.1 71.6 all-gather.4
  1059.1 190.4 reduce-scatter.4
  1252.1 30.3 all-reduce.5
  1285.6 349.7 all-reduce.7
where the time goes:
time: 1670 us; the launch traced here: 1640 us
  waiting for transfers between devices  867 us (52%)
  other arithmetic  231 us (14%)
  matrix products  191 us (11%)
  local copies, waits for them, and re-layouts  145 us (9%)
  loops' own time  126 us (8%)
  blocking collectives  68.3 us (4%)
    reduce_scatter x2, waiting for transfers between devices, collect(): lax.psum_scatter(entity_terms(messages, jnp.int32(0)), 'ent', scatter_dim...  379 us
    psum x1, waiting for transfers between devices, body(): grad_theta = lax.psum(local_theta, 'ent')  349 us
    another operation x2, loops' own time, entity_terms(): pieces = lax.map(block_term, jnp.arange(block_span, dtype=jnp.int32))  125 us
    scatter-add x1, other arithmetic, body(): jax.ops.segment_sum(usable_float.reshape(-1), entity_index.reshape(-1), n...  113 us
    scatter-add x1, other arithmetic, body(): jax.ops.segment_sum(usable_float.reshape(-1), row_lists.reshape(-1), num_...  113 us
    dot_general x64, matrix products, add_block(): jnp.einsum('ps,pf->sf', row_hot, picked, preferred_element_type=jnp.float32)  108 us
    dot_general x64, matrix products, block_term(): jnp.einsum('pw,pf->wf', col_hot, picked, preferred_element_type=jnp.float32)  77.7 us
    all_gather x1, waiting for transfers between devices, body(): lax.all_gather(back_scaled, 'ent', axis=0, tiled=True)  73.9 us
  transfers between devices with their start and end apart: 7, of which 6 were waited for; matrix products, arithmetic and copies ran while one was open for 7% of the time, Pallas kernels for 0%

commit v1 on v0

--- a/solution.py
+++ b/solution.py
@@ -24,7 +24,7 @@
     local_degree = jax.ops.segment_sum(
         usable_float.reshape(-1), entity_index.reshape(-1), num_segments=blocks_count * ent_dev
     )
-    entity_degree = lax.psum(local_degree, ("ent", "sec"))
+    entity_degree = lax.psum(lax.psum(local_degree, "ent"), "sec")
     own_degree = lax.dynamic_slice_in_dim(entity_degree, own_block * ent_dev, ent_dev)
     entity_scale = lax.rsqrt(1.0 + own_degree)[:, None]
     sec_count = jax.ops.segment_sum(

time: 1670 us -> 1790 us (1.072)
  blocking collectives: 68.3 us -> 195 us
    psum x1 -> x2, blocking collectives: 68.3 us -> 195 us  [body(): entity_degree = lax.psum(lax.psum(local_degree, 'ent'), 'sec')]
where the time goes in v1:
time: 1790 us; the launch traced here: 1770 us
  waiting for transfers between devices  866 us (48%)
  other arithmetic  231 us (13%)
  blocking collectives  195 us (11%)
  matrix products  191 us (11%)
  local copies, waits for them, and re-layouts  145 us (8%)
  loops' own time  126 us (7%)
    reduce_scatter x2, waiting for transfers between devices, collect(): lax.psum_scatter(entity_terms(messages, jnp.int32(0)), 'ent', scatter_dim...  378 us
    psum x1, waiting for transfers between devices, body(): grad_theta = lax.psum(local_theta, 'ent')  349 us
    psum x2, blocking collectives, body(): entity_degree = lax.psum(lax.psum(local_degree, 'ent'), 'sec')  195 us
    another operation x2, loops' own time, entity_terms(): pieces = lax.map(block_term, jnp.arange(block_span, dtype=jnp.int32))  125 us
    scatter-add x1, other arithmetic, body(): jax.ops.segment_sum(usable_float.reshape(-1), entity_index.reshape(-1), n...  113 us
    scatter-add x1, other arithmetic, body(): jax.ops.segment_sum(usable_float.reshape(-1), row_lists.reshape(-1), num_...  113 us
    dot_general x64, matrix products, add_block(): jnp.einsum('ps,pf->sf', row_hot, picked, preferred_element_type=jnp.float32)  108 us
    dot_general x64, matrix products, block_term(): jnp.einsum('pw,pf->wf', col_hot, picked, preferred_element_type=jnp.float32)  77.7 us
  transfers between devices with their start and end apart: 7, of which 6 were waited for; matrix products, arithmetic and copies ran while one was open for 7% of the time, Pallas kernels for 0%

profile of v1, /device:TPU:0, one launch (start us, length us, event | category | flops | bytes accessed | tf_op | source)
XLA Modules:
  0.0 1769.7 jit_solution(4529939575746908768)
XLA Ops:
  9.2 113.5 %scatter_custom_fusion = f32[4096]{0:T(1024)S(1)} fusion(s32[16384]{0:T(1024)S(1)} %bitcast.81, f32[16384]{0:T(1024)S(1)} %bitcast.82, f32[]{:T(128)} %constant.131.clone.1), kind=kCustom, calls=%fused_computation.76 | custom fusion | flops 16384 | bytes 16388 | tf_op jit(solution)/shard_map/scatter-add | solution.py:24
  122.6 185.2 %psum.35 = f32[4096]{0:T(1024)S(1)} all-reduce(f32[4096]{0:T(1024)S(1)} %scatter_custom_fusion), channel_id=1, replica_groups=mesh['ent'=32,'sec'=4] {'ent'}, use_global_device_ids=true, to_apply=%region_1.0 | all-reduce | flops 4096 | bytes 32768 | tf_op jit(solution)/shard_map/psum | solution.py:27
  307.8 10.3 psum.36
  320.7 113.4 %scatter_custom_fusion.1 = f32[512]{0:T(512)S(1)} fusion(s32[16384]{0:T(1024)S(1)} %bitcast.84, f32[16384]{0:T(1024)S(1)} %bitcast.83, f32[]{:T(128)} %constant.137.clone.1), kind=kCustom, calls=%fused_computation.78 | custom fusion | flops 16384 | bytes 2052 | tf_op jit(solution)/shard_map/scatter-add | solution.py:30
  434.8 79.9 %while.50 = (s32[]{:T(128)}, f32[512,256]{1,0:T(8,128)S(1)}, s32[32,512]{1,0:T(8,128)}, pred[32,512]{1,0:T(8,128)(4,1)S(1)}, s32[32,512]{1,0:T(8,128)}, /*index=...) while((s32[]{:T(128)}, f32[512,256]{1,0:T(8,128)S(1)}, ...), condition=%wide.region_5.6_spmd.clone, body=%wide.region_4.5_spmd.clone.sunk | while | flops 168820736 | bytes 1128617 | solution.py:55
  445.6 1.7 convolution_add_fusion.4
  448.1 1.7 convolution_add_fusion.4
  463.1 1.7 convolution_add_fusion.4
  465.6 1.7 convolution_add_fusion.4
  480.6 1.7 convolution_add_fusion.4
  483.1 1.7 convolution_add_fusion.4
  498.1 1.7 convolution_add_fusion.4
  500.6 1.7 convolution_add_fusion.4
  514.9 2.4 broadcast.21.clone
  517.3 144.5 %while.48 = (s32[]{:T(128)}, f32[32,128,256]{2,1,0:T(8,128)}, s32[32]{0:T(128)S(1)}, s32[32,512]{1,0:T(8,128)}, pred[32,512]{1,0:T(8,128)(4,1)S(1)}, /*index=5*/...) while((s32[]{:T(128)}, f32[32,128,256]{2,1,0:T(8,128)}, ...), condition=%wide.region_7.8_spmd, body=%wide.region_6.7_spmd.sunk | while | flops 168558592 | bytes 408219 | solution.py:73
  661.9 186.8 %reduce-scatter.3.cloned.1.call-done = f32[128,256]{1,0:T(8,128)} async-done(((f32[4096,256]{1,0:T(8,128)}), f32[128,256]{1,0:T(8,128)}) %reduce-scatter.3.cloned.1.call-update) | async-done | bytes 131088 | tf_op jit(solution)/shard_map/reduce_scatter | solution.py:77
  848.8 32.8 %all-reduce.4.cloned.1.call-done = f32[128,256]{1,0:T(8,128)} async-done(((f32[128,256]{1,0:T(8,128)}), f32[128,256]{1,0:T(8,128)}) %all-reduce.4.cloned.1.call-update) | async-done | bytes 131088 | tf_op jit(solution)/shard_map/psum | solution.py:80
  881.6 1.7 multiply_convert_fusion.3
  883.4 73.9 %all-gather.5.cloned.1.call-done = bf16[4096,256]{1,0:T(8,128)(2,1)} async-done(((bf16[128,256]{1,0:T(8,128)(2,1)}), bf16[4096,256]{1,0:T(8,128)(2,1)}) %all-gather.5.cloned.1.call-update) | async-done | bytes 2097168 | tf_op jit(solution)/shard_map/all_gather | solution.py:96
  957.3 79.9 %while.51 = (s32[]{:T(128)}, f32[512,256]{1,0:T(8,128)S(1)}, s32[32,512]{1,0:T(8,128)}, pred[32,512]{1,0:T(8,128)(4,1)S(1)}, s32[32,512]{1,0:T(8,128)}, /*index=...) while((s32[]{:T(128)}, f32[512,256]{1,0:T(8,128)S(1)}, ...), condition=%wide.region_11.12_spmd.clone, body=%wide.region_10.11_spmd.clone.sunk | while | flops 168820736 | bytes 1128617 | solution.py:55
  970.5 1.7 convolution_add_fusion.5
  973.0 1.7 convolution_add_fusion.5
  988.0 1.7 convolution_add_fusion.5
  990.5 1.7 convolution_add_fusion.5
  1037.4 2.4 broadcast.21
  1039.9 144.5 %while.49 = (s32[]{:T(128)}, f32[32,128,256]{2,1,0:T(8,128)}, s32[32]{0:T(128)S(1)}, s32[32,512]{1,0:T(8,128)}, pred[32,512]{1,0:T(8,128)(4,1)S(1)}, /*index=5*/...) while((s32[]{:T(128)}, f32[32,128,256]{2,1,0:T(8,128)}, ...), condition=%wide.region_13.14_spmd, body=%wide.region_12.13_spmd.sunk | while | flops 168558592 | bytes 408219 | solution.py:73
  1184.4 190.9 %reduce-scatter.5.cloned.1.call-done = f32[128,256]{1,0:T(8,128)} async-done(((f32[4096,256]{1,0:T(8,128)}), f32[128,256]{1,0:T(8,128)}) %reduce-scatter.5.cloned.1.call-update) | async-done | bytes 131088 | tf_op jit(solution)/shard_map/reduce_scatter | solution.py:77
  1375.5 32.7 %all-reduce.6.cloned.1.call-done = f32[128,256]{1,0:T(8,128)} async-done(((f32[128,256]{1,0:T(8,128)}), f32[128,256]{1,0:T(8,128)}) %all-reduce.6.cloned.1.call-update) | async-done | bytes 131088 | tf_op jit(solution)/shard_map/psum | solution.py:80
  1408.2 1.9 convolution_bitcast_fusion
  1410.7 1.7 convolution_convert_fusion.4
  1412.4 348.6 %all-reduce.8.cloned.1.call-done = f32[256,256]{0,1:T(8,128)} async-done(((f32[256,256]{0,1:T(8,128)}), f32[256,256]{0,1:T(8,128)}) %all-reduce.8.cloned.1.call-update) | async-done | bytes 262160 | tf_op jit(solution)/shard_map/psum | solution.py:108
  1761.1 1.8 copy.11
  (475 shorter events, 308.7 us)
Async XLA Ops:
  7.2 311.0 %copy-start = (bf16[256,256]{1,0:T(8,128)(2,1)S(1)}, bf16[256,256]{1,0:T(8,128)(2,1)}, u32[]{:S(2)}) copy-start(bf16[256,256]{1,0:T(8,128)(2,1)} %param.16) | copy-start | bytes 393220
  7.2 427.7 %all-gather.3.cloned.1.call-start = ((), (), s32[]{:S(2)}) async-start(), calls=%async_computation.2 | async-start | bytes 2162688 | tf_op jit(solution)/shard_map/all_gather | solution.py:86
  319.8 529.0 %reduce-scatter.3.cloned.1.call-start = ((), (), s32[]{:S(2)}) async-start(), calls=%async_computation.3 | async-start | bytes 4325376 | tf_op jit(solution)/shard_map/reduce_scatter | solution.py:77
  517.3 364.3 %copy-start.2 = (bf16[128,256]{1,0:T(8,128)(2,1)S(1)}, bf16[128,256]{1,0:T(8,128)(2,1)}, u32[]{:S(2)}) copy-start(bf16[128,256]{1,0:T(8,128)(2,1)} %param.21) | copy-start | bytes 196612
  661.9 219.7 %all-reduce.4.cloned.1.call-start = ((), (), s32[]{:S(2)}) async-start(), calls=%async_computation.4 | async-start | bytes 262144 | tf_op jit(solution)/shard_map/psum | solution.py:80
  848.8 108.5 %all-gather.5.cloned.1.call-start = ((), (), s32[]{:S(2)}) async-start(), calls=%async_computation.5 | async-start | bytes 2162688 | tf_op jit(solution)/shard_map/all_gather | solution.py:96
  883.3 492.1 %reduce-scatter.5.cloned.1.call-start = ((), (), s32[]{:S(2)}) async-start(), calls=%async_computation.6 | async-start | bytes 4325376 | tf_op jit(solution)/shard_map/reduce_scatter | solution.py:77
  1039.8 368.3 %copy-start.1 = (bf16[128,256]{1,0:T(8,128)(2,1)S(1)}, bf16[128,256]{1,0:T(8,128)(2,1)}, u32[]{:S(2)}) copy-start(bf16[128,256]{1,0:T(8,128)(2,1)} %param.15) | copy-start | bytes 196612
  1184.4 223.8 %all-reduce.6.cloned.1.call-start = ((), (), s32[]{:S(2)}) async-start(), calls=%async_computation.7 | async-start | bytes 262144 | tf_op jit(solution)/shard_map/psum | solution.py:80
  1375.4 385.7 %all-reduce.8.cloned.1.call-start = ((), (), s32[]{:S(2)}) async-start(), calls=%async_computation.8 | async-start | bytes 524288 | tf_op jit(solution)/shard_map/psum | solution.py:108
Sparse Core Ops, SparseCore 0:
  319.9 65.0 all-gather.2
  662.0 186.7 reduce-scatter.2
  851.2 30.3 all-reduce.3
  885.5 71.6 all-gather.4
  1184.5 190.8 reduce-scatter.4
  1377.9 30.2 all-reduce.5
  1411.2 349.7 all-reduce.7
